TPU v7x, 32 devices: a whole 2x2x4 slice. The times are simulated.
32 devices in a mesh: tm: 16 (over z, y, x), head: 2 (over core).
Axes of the slice: x: 2, y: 2, z: 4, core: 2. Of those that a mesh axis runs over, the one named last changes fastest.
Arguments:
- patches: bfloat16 [192, 256, 1152], P('tm', None, 'head'), may hold values from -6 to 6
- grid_rows: int32 [192], P('tm'), may hold values from 8 to 16
- frame_ids: int32 [192], P('tm'), may hold values from 0 to 191, as said below
- ln_gain: float32 [1152], replicated, may hold values from 0.1 to 1.9
- w_qkv: bfloat16 [3, 1152, 1152], P(None, None, 'head'), may hold values from -5.9514821 to 5.9514821
- w_out: bfloat16 [1152, 1152], P('head'), may hold values from -0.1875 to 0.1875
- w_conn: bfloat16 [1152, 4096], P(None, 'head'), may hold values from -0.1875 to 0.1875
- norm_gain: float32 [4096], replicated, may hold values from 0.1 to 1.9
- w_x: bfloat16 [4096, 4096], P(None, 'head'), may hold values from -0.09375 to 0.09375
- w_b: bfloat16 [4096, 1024], P(None, 'head'), may hold values from -0.09375 to 0.09375
- w_c: bfloat16 [4096, 1024], P(None, 'head'), may hold values from -0.09375 to 0.09375
- w_dt: bfloat16 [4096, 64], P(None, 'head'), may hold values from -0.09375 to 0.09375
- dt_bias: float32 [64], P('head'), may hold values from -1 to 1
- a_log: float32 [64], P('head'), may hold values from -14 to -3.2
- d_skip: float32 [64], P('head'), may hold values from 0.5 to 1.5
- out_gain: float32 [4096], P('head'), may hold values from 0.1 to 1.9
Outputs:
- stream: bfloat16 [12288, 4096], P('tm', 'head')
- ssd_out: bfloat16 [12288, 4096], P('tm', 'head')
Inputs may be any that keep to these rules, and one draw needn't show every extreme that they name: frame_ids is a permutation of the frames; the 12 slots of one tm index hold frames of 12 different time shards, time shard of a frame being frame // 12.
All inputs are finite; a program needn't handle non-finite values.
Results may differ from a plain program's by a relative error of at most 0.013.
Values may be sent and summed in bfloat16 or wider, within the bound.
A program may use at most 128 MiB of HBM per device.

v0:
```python
import jax
import jax.numpy as jnp
from jax import lax
from jax.sharding import PartitionSpec as P

GRID = 16
POOL = 4
VHD = 72
HDIM = 64
STATE = 128
STRETCH = 256
highest = lax.Precision.HIGHEST


def carried_in(value, axis, combine, identity):
    count, position = (lax.axis_size(axis), lax.axis_index(axis))
    everything = jax.tree.map(
        lambda part, kind: lax.all_gather(part.astype(kind), axis),
        value,
        (jnp.bfloat16, jnp.bfloat16),
    )
    start = jax.tree.map(
        lambda part, zero: jnp.broadcast_to(jnp.asarray(zero, part.dtype), part.shape),
        value,
        identity,
    )

    def step(k, before):
        reached = k < position
        new = combine(
            before, jax.tree.map(lambda part, own: part[k].astype(own.dtype), everything, value)
        )
        return jax.tree.map(lambda a, b: jnp.where(reached, a, b), new, before)

    return lax.fori_loop(0, count, step, start)


def layer_norm(rows, gain):
    values = rows.astype(jnp.float32)
    centre = jnp.mean(values, axis=-1, keepdims=True)
    spread = jnp.mean(jnp.square(values - centre), axis=-1, keepdims=True)
    return ((values - centre) * lax.rsqrt(spread + 1e-06) * gain).astype(jnp.bfloat16)


def attend(full_patches, valid_count, ln_gain, w_qkv, w_out):
    frame_count, patch_count, full_width = full_patches.shape
    local_width = w_qkv.shape[2]
    local_heads = local_width // VHD
    normed = layer_norm(full_patches, ln_gain).reshape(frame_count * patch_count, full_width)
    triple = jnp.einsum("rc,mcd->mrd", normed, w_qkv, preferred_element_type=jnp.float32).astype(
        jnp.bfloat16
    )
    triple = triple.reshape(3, frame_count, patch_count, local_heads, VHD)
    scores = jnp.einsum(
        "fqhd,fkhd->fhqk", triple[0], triple[1], preferred_element_type=jnp.float32
    ) * VHD ** (-0.5)
    usable = jnp.arange(patch_count)[None, :] < valid_count[:, None]
    scores = jnp.where(usable[:, None, None, :], scores, -1e30)
    row_max = jnp.max(scores, axis=-1, keepdims=True)
    powered = jnp.exp(scores - row_max)
    weights_soft = (powered / jnp.sum(powered, axis=-1, keepdims=True)).astype(jnp.bfloat16)
    context = jnp.einsum(
        "fhqk,fkhd->fqhd", weights_soft, triple[2], preferred_element_type=jnp.float32
    ).astype(jnp.bfloat16)
    attended = jnp.dot(
        context.reshape(frame_count * patch_count, local_width),
        w_out,
        preferred_element_type=jnp.float32,
    )
    return jnp.mean(attended.reshape(frame_count, patch_count // POOL, POOL, full_width), axis=2)


def bucket_frames(owned, frame_ids, shards):
    frame_count = owned.shape[0]
    target = frame_ids // frame_count
    onehot = target[None, :] == jnp.arange(shards)[:, None]
    outgoing = jnp.einsum(
        "tf,fpc->tpc", onehot.astype(owned.dtype), owned, preferred_element_type=jnp.float32
    ).astype(owned.dtype)
    labels = jnp.sum(jnp.where(onehot, frame_ids[None, :] + 1, 0), axis=1)
    return (outgoing, labels)


def place_frames(incoming, arrived, frame_count):
    first_frame = lax.axis_index("tm") * frame_count
    local_frame = arrived - 1 - first_frame
    onehot = jnp.arange(frame_count)[:, None] == local_frame[None, :]
    placed = jnp.einsum(
        "ft,tpc->fpc", onehot.astype(incoming.dtype), incoming, preferred_element_type=jnp.float32
    ).astype(incoming.dtype)
    return placed.reshape(frame_count * incoming.shape[1], incoming.shape[2])


def project(stream_rows, norm_gain, w_x, w_b, w_c, w_dt, dt_bias, a_log):
    values = stream_rows.astype(jnp.float32)
    normed = (
        values * lax.rsqrt(jnp.mean(values * values, axis=-1, keepdims=True) + 1e-05) * norm_gain
    ).astype(jnp.bfloat16)
    inner_rows = jnp.dot(normed, w_x, preferred_element_type=jnp.float32).astype(jnp.bfloat16)
    write_keys = jnp.dot(normed, w_b, preferred_element_type=jnp.float32).astype(jnp.bfloat16)
    read_keys = jnp.dot(normed, w_c, preferred_element_type=jnp.float32).astype(jnp.bfloat16)
    step_size = jax.nn.softplus(jnp.dot(normed, w_dt, preferred_element_type=jnp.float32) + dt_bias)
    log_decay = -jnp.exp(a_log) * step_size
    return (inner_rows, write_keys, read_keys, step_size, log_decay)


def ssd_stretch(inner_rows, write_keys, read_keys, step_size, log_decay, d_skip, state):
    length = inner_rows.shape[0]
    head_count = step_size.shape[1]
    groups = write_keys.shape[1] // STATE
    per_group = head_count // groups
    cumul = jnp.cumsum(log_decay, axis=0)
    scaled = (
        inner_rows.astype(jnp.float32).reshape(length, head_count, HDIM) * step_size[:, :, None]
    )
    writers = write_keys.astype(jnp.float32).reshape(length, groups, STATE)
    readers = read_keys.astype(jnp.float32).reshape(length, groups, STATE)
    intersection = jnp.einsum("tgn,sgn->gts", readers, writers, precision=highest)
    causal = (jnp.arange(length)[:, None] >= jnp.arange(length)[None, :])[:, :, None]
    spans = cumul[:, None, :] - cumul[None, :, :]
    decays = jnp.where(causal, jnp.exp(jnp.where(causal, spans, 0.0)), 0.0)
    mixing = jnp.repeat(intersection, per_group, axis=0) * jnp.transpose(decays, (2, 0, 1))
    within = jnp.einsum("hts,shp->thp", mixing, scaled, precision=highest)
    carried = (
        jnp.einsum(
            "tgn,gkpn->tgkp",
            readers,
            state.reshape(groups, per_group, HDIM, STATE),
            precision=highest,
        ).reshape(length, head_count, HDIM)
        * jnp.exp(cumul)[:, :, None]
    )
    remaining = jnp.exp(cumul[-1][None, :] - cumul)
    fresh_state = jnp.einsum(
        "sgkp,sgn->gkpn",
        (scaled * remaining[:, :, None]).reshape(length, groups, per_group, HDIM),
        writers,
        precision=highest,
    ).reshape(head_count, HDIM, STATE)
    new_state = jnp.exp(cumul[-1])[:, None, None] * state + fresh_state
    outputs = (
        within
        + carried
        + d_skip[None, :, None] * inner_rows.astype(jnp.float32).reshape(length, head_count, HDIM)
    )
    return (outputs, new_state, cumul)


def group_norm(outputs, out_gain, groups):
    length = outputs.shape[0]
    grouped = outputs.reshape(length, groups, -1)
    normed = grouped * lax.rsqrt(jnp.mean(grouped * grouped, axis=-1, keepdims=True) + 1e-05)
    return (normed.reshape(length, -1) * out_gain).astype(jnp.bfloat16)


def combine_states(earlier, later):
    return (earlier[0] + later[0], jnp.exp(later[0])[:, None, None] * earlier[1] + later[1])


def on_device(
    patches,
    grid_rows,
    frame_ids,
    ln_gain,
    w_qkv,
    w_out,
    w_conn,
    norm_gain,
    w_x,
    w_b,
    w_c,
    w_dt,
    dt_bias,
    a_log,
    d_skip,
    out_gain,
):
    frame_count, patch_count, slice_width = patches.shape
    tokens_frame = patch_count // POOL
    shards = lax.axis_size("tm")
    full_patches = lax.all_gather(patches, "head", axis=2, tiled=True)
    full_width = full_patches.shape[2]
    valid_count = grid_rows * GRID
    attn_pooled = attend(full_patches, valid_count, ln_gain, w_qkv, w_out)
    kept_tokens = (jnp.arange(tokens_frame)[None, :] * POOL < valid_count[:, None])[:, :, None]
    summed_attn = lax.psum(attn_pooled, "head")
    pooled_patches = jnp.mean(
        full_patches.astype(jnp.float32).reshape(frame_count, tokens_frame, POOL, full_width),
        axis=2,
    )
    vision = jnp.where(kept_tokens, pooled_patches + summed_attn, 0.0).astype(jnp.bfloat16)
    projected = jnp.dot(
        vision.reshape(frame_count * tokens_frame, full_width),
        w_conn,
        preferred_element_type=jnp.float32,
    ).astype(jnp.bfloat16)
    outgoing, labels = bucket_frames(
        projected.reshape(frame_count, tokens_frame, w_conn.shape[1]), frame_ids, shards
    )
    incoming, arrived = (
        lax.all_to_all(outgoing, "tm", split_axis=0, concat_axis=0, tiled=True),
        lax.all_to_all(labels, "tm", split_axis=0, concat_axis=0, tiled=True),
    )
    stream_rows = place_frames(incoming, arrived, frame_count)
    wide = lax.all_gather(stream_rows, "head", axis=1, tiled=True)
    token_count = wide.shape[0]
    local_heads = w_dt.shape[1]
    groups = w_b.shape[1] // STATE
    per_group = local_heads // groups
    projected_rows = project(wide, norm_gain, w_x, w_b, w_c, w_dt, dt_bias, a_log)
    stretch_count = token_count // STRETCH
    sliced = tuple(
        (member.reshape(stretch_count, STRETCH, member.shape[1]) for member in projected_rows)
    )

    def stretch_step(state, pieces):
        outputs, new_state, cumul = ssd_stretch(
            pieces[0], pieces[1], pieces[2], pieces[3], pieces[4], d_skip, state
        )
        return (new_state, (outputs, cumul))

    zero_state = jnp.zeros((local_heads, HDIM, STATE), jnp.float32)
    device_state, (outputs, cumul) = lax.scan(stretch_step, zero_state, sliced)
    totals = cumul[:, -1, :]
    total_log = jnp.sum(totals, axis=0)
    identity = (jnp.zeros_like(total_log), jnp.zeros_like(device_state))
    incoming_state = carried_in((total_log, device_state), "tm", combine_states, identity)[1]
    offsets = jnp.cumsum(totals, axis=0) - totals
    from_start = (cumul + offsets[:, None, :]).reshape(token_count, local_heads)
    readers = projected_rows[2].astype(jnp.float32).reshape(token_count, groups, STATE)
    correction = (
        jnp.einsum(
            "tgn,gkpn->tgkp",
            readers,
            incoming_state.reshape(groups, per_group, HDIM, STATE),
            precision=highest,
        ).reshape(token_count, local_heads, HDIM)
        * jnp.exp(from_start)[:, :, None]
    )
    combined = outputs.reshape(token_count, local_heads, HDIM) + correction
    return (stream_rows, group_norm(combined, out_gain, groups))


def solution(mesh):
    in_specs = (
        P("tm", None, "head"),
        P("tm"),
        P("tm"),
        P(),
        P(None, None, "head"),
        P("head", None),
        P(None, "head"),
        P(),
        P(None, "head"),
        P(None, "head"),
        P(None, "head"),
        P(None, "head"),
        P("head"),
        P("head"),
        P("head"),
        P("head"),
    )
    out_specs = (P("tm", "head"), P("tm", "head"))
    return jax.shard_map(
        on_device, mesh=mesh, in_specs=in_specs, out_specs=out_specs, check_vma=False
    )
```

profile of v0, /device:TPU:0, one launch (start us, length us, event | category | flops | bytes accessed | tf_op | source)
XLA Modules:
  0.0 784.5 jit_solution(12642048657780200994)
XLA Ops:
  8.7 21.5 %all-gather.6.cloned.1.call-done = bf16[12,256,1152]{1,2,0:T(8,128)(2,1)} async-done(((bf16[12,256,576]{1,2,0:T(8,128)(2,1)}), bf16[12,256,1152]{1,2,0:T(8,128)(2,1)}) %all-gather.6.cloned.1.call-update) | async-done | bytes 7077904 | tf_op jit(solution)/shard_map/all_gather | solution.py:181
  30.2 10.3 %copy.121 = bf16[12,256,1152]{2,1,0:T(8,128)(2,1)} copy(bf16[12,256,1152]{1,2,0:T(8,128)(2,1)} %all-gather.6.cloned.1.call-done) | data formatting | bytes 14155776 | tf_op jit(solution)/shard_map/all_gather | solution.py:181
  40.5 4.2 convert_reduce_fusion
  45.6 2.0 multiply_reduce_fusion
  47.6 2.4 multiply_convert_fusion
  50.0 15.7 %convert_bitcast_fusion = bf16[3,3072,576]{1,2,0:T(8,128)(2,1)S(1)} fusion(bf16[3072,1152,1]{1,0,2:T(8,128)(2,1)S(1)} %bitcast.239, bf16[3,1152,576]{1,2,0:T(8,128)(2,1)} %param.24), kind=kOutput, calls=%fused_computation.52 | convolution fusion | flops 12235898880 | bytes 21676032 | tf_op jit(solution)/shard_map/rc,mcd->mrd/dot_general | solution.py:50
  65.7 4.1 fusion.96
  69.9 7.2 squeeze.32
  77.1 7.3 squeeze.33
  84.5 7.2 squeeze.31
  91.7 15.7 %fusion.97 = f32[12,8,256]{2,1,0:T(8,128)S(1)} fusion(pred[12,256]{1,0:T(8,128)(4,1)S(1)} %iota_compare_fusion.1, bf16[12,256,8,72]{1,0,3,2:T(8,128)(2,1)} %squeeze.33, bf16[12,256,8,72]{1,0,3,2:T(8,128)(2,1)} %squeeze.32), kind=kOutput, calls=%fused_computation.120 | convolution fusion | flops 931135744 | bytes 7179264 | tf_op jit(solution)/shard_map/sub | solution.py:60
  107.4 21.9 %convert_bitcast_fusion.1 = bf16[12,256,8,72]{1,3,2,0:T(8,128)(2,1)} fusion(f32[12,8,256]{2,1,0:T(8,128)S(1)} %fusion.97, pred[12,256]{1,0:T(8,128)(4,1)S(1)} %iota_compare_fusion.1, bf16[12,256,8,72]{1,0,3,2:T(8,128)(2,1)} %squeeze.31, bf16[12,256,8,72]{1,0,3,2:T(8,128)(2,1)} %squeeze.33, bf16[12,256,8,72]{1,0,3,2:T(8,128)(2,1)} %squeeze.32), kind=kOutput, calls=%fused_computation.71 | convolution fusion | flops 1845190912 | bytes 14257152 | tf_op jit(solution)/shard_map/fhqk,fkhd->fqhd/dot_general | solution.py:62
  129.3 8.0 %copy.126 = bf16[12,256,8,72]{3,2,1,0:T(8,128)(2,1)} copy(bf16[12,256,8,72]{1,3,2,0:T(8,128)(2,1)} %convert_bitcast_fusion.1) | data formatting | bytes 7077888 | tf_op jit(solution)/shard_map/convert_element_type | solution.py:64
  137.3 11.6 %dot_general.53 = bf16[12,64,4,576]{3,2,1,0:T(4,128)(2,1)} reshape(bf16[12,256,8,72]{3,2,1,0:T(8,128)(2,1)} %copy.126) | data formatting | bytes 7077888 | tf_op jit(solution)/shard_map/dot_general | solution.py:65
  148.9 8.6 %fusion.49 = f32[12,64,1152]{2,1,0:T(8,128)S(1)} fusion(bf16[12,64,4,576]{3,2,1,0:T(4,128)(2,1)} %dot_general.53, bf16[576,1152]{1,0:T(8,128)(2,1)S(1)} %copy-done), kind=kOutput, calls=%fused_computation.74 | convolution fusion | flops 4079517696 | bytes 8404992 | tf_op jit(solution)/shard_map/dot_general | solution.py:65
  157.6 2.2 broadcast_multiply_fusion
  160.7 6.8 all-to-all-start
  167.5 14.0 %reshape.268 = f32[12,64,4,1152]{3,2,1,0:T(4,128)} reshape(bf16[12,256,1152]{2,1,0:T(8,128)(2,1)} %copy.121) | data formatting | bytes 21233664 | tf_op jit(solution)/shard_map/reshape | solution.py:188
  181.5 13.0 %reduce_sum.89 = f32[12,64,1152]{2,1,0:T(8,128)} reduce(f32[12,64,4,1152]{3,2,1,0:T(4,128)} %reshape.268, f32[]{:T(128)} %constant.94.clone.1), dimensions={2}, to_apply=%region_1.0 | reduce | flops 2654208 | bytes 17694724 | tf_op jit(solution)/shard_map/reduce_sum | solution.py:187
  194.5 3.5 select_convert_fusion
  198.0 6.9 convolution_convert_fusion.1
  204.9 2.3 fusion.38
  207.2 4.3 copy.129
  211.5 7.0 all-to-all-start.1
  218.9 79.3 %all-to-all-done.1 = bf16[16,64,2048]{2,1,0:T(8,128)(2,1)} async-done(((bf16[16,64,2048]{2,1,0:T(8,128)(2,1)}), bf16[16,64,2048]{2,1,0:T(8,128)(2,1)}, u32[]{:S(2)}, u32[]{:S(2)}) %all-to-all-start.1) | async-done | bytes 4194336 | tf_op jit(solution)/shard_map/all_to_all | solution.py:201
  298.2 7.0 fusion.41
  305.2 3.4 copy.131
  308.9 31.1 %all-gather.8.cloned.1.call-done = bf16[768,4096]{1,0:T(8,128)(2,1)} async-done(((bf16[768,2048]{1,0:T(8,128)(2,1)}), bf16[768,4096]{1,0:T(8,128)(2,1)}) %all-gather.8.cloned.1.call-update) | async-done | bytes 6291472 | tf_op jit(solution)/shard_map/all_gather | solution.py:205
  340.0 4.2 fusion.19
  344.6 2.1 broadcast_multiply_fusion.1
  346.9 8.5 %convolution_convert_fusion.2 = bf16[768,512]{1,0:T(8,128)(2,1)} fusion(bf16[4096,512]{1,0:T(8,128)(2,1)} %param.30, bf16[768,4096]{1,0:T(8,128)(2,1)} %all-gather.8.cloned.1.call-done, f32[4096]{0:T(1024)S(1)} %copy-done.13, f32[768]{0:T(1024)S(1)} %add_rsqrt_fusion.2), kind=kOutput, calls=%fused_computation.83 | convolution fusion | flops 3234201600 | bytes 11291648 | tf_op jit(solution)/shard_map/dot_general | solution.py:101
  355.4 4.4 convolution_convert_fusion.3
  359.8 17.9 %convolution_convert_fusion = bf16[768,2048]{1,0:T(8,128)(2,1)} fusion(bf16[4096,2048]{1,0:T(8,128)(2,1)} %param.28, bf16[768,4096]{1,0:T(8,128)(2,1)S(1)} %bitcast.241, f32[4096]{0:T(1024)S(1)} %copy-done.13, f32[768]{0:T(1024)S(1)} %add_rsqrt_fusion.2), kind=kOutput, calls=%fused_computation.72 | convolution fusion | flops 12899057664 | bytes 26233856 | tf_op jit(solution)/shard_map/dot_general | solution.py:99
  377.8 225.2 %while.29 = (s32[]{:T(128)}, f32[32,64,128]{2,1,0:T(8,128)}, f32[3,256,32,64]{1,0,3,2:T(4,128)}, f32[3,256,32]{1,2,0:T(8,128)}, f32[3,256,32]{1,0,2:T(4,128)S(1)...) while((s32[]{:T(128)}, f32[32,64,128]{2,1,0:T(8,128)}, ...), condition=%wide.region_12.13_spmd.clone, body=%wide.region_9.12_spmd.clone.sunk | while | flops 3302842368 | bytes 56987660 | solution.py:223
  384.0 2.9 fusion.146
  386.9 2.4 bitcast_add_fusion.2
  391.2 1.9 fusion.147
  394.4 1.9 bitcast_multiply_fusion.4
  396.3 8.0 %fusion.149 = f32[1,256,32,64]{1,3,2,0:T(8,128)S(1)} fusion(f32[256,32,64]{0,2,1:T(8,128)S(1)} %bitcast.224, f32[4,256,8,64]{1,3,2,0:T(8,128)S(1)} %fusion.147, f32[32,256,256]{2,1,0:T(8,128)S(1)} %bitcast_multiply_fusion.4, f32[32]{0:T(128)S(1)} %get-tuple-element.461, f32[256,32]{0,1:T(8,128)S(1)} %get-tuple-element.420, f32[256,32]{0,1:T(8,128)S(1)} %bitcast.238), kind=kOutput, calls=%fused_computation.12.clone.1 | convolution fusion | flops 1613234176 | bytes 14745728 | tf_op jit(solution)/shard_map/while/body/eval_jaxpr/hts,shp->thp/dot_general | solution.py:123
  404.4 2.2 copy.261
  406.5 45.6 %dynamic_update_slice.14 = f32[3,256,32,64]{1,0,3,2:T(4,128)} dynamic-update-slice(f32[3,256,32,64]{1,0,3,2:T(4,128)} %get-tuple-element.441, f32[1,256,32,64]{1,0,3,2:T(1,128)S(1)} %copy.261, s32[]{:T(128)} %get-tuple-element.439, s32[]{:T(128)} %constant.88.clone.1..sunk, s32[]{:T(128)} %constant.88.clone.1..sunk, s32[]{:T(128)} %constant.88.clone.1..sunk) | dynamic-update-slice | bytes 4194308 | tf_op jit(solution)/shard_map/while/body/jit(dynamic_update_index_in_dim)/dynamic_update_slice | solution.py:223
  458.7 2.9 fusion.146
  461.6 2.7 bitcast_add_fusion.2
  466.1 1.9 fusion.147
  469.4 1.9 bitcast_multiply_fusion.4
  471.3 8.0 %fusion.149 = f32[1,256,32,64]{1,3,2,0:T(8,128)S(1)} fusion(f32[256,32,64]{0,2,1:T(8,128)S(1)} %bitcast.224, f32[4,256,8,64]{1,3,2,0:T(8,128)S(1)} %fusion.147, f32[32,256,256]{2,1,0:T(8,128)S(1)} %bitcast_multiply_fusion.4, f32[32]{0:T(128)S(1)} %get-tuple-element.461, f32[256,32]{0,1:T(8,128)S(1)} %get-tuple-element.420, f32[256,32]{0,1:T(8,128)S(1)} %bitcast.238), kind=kOutput, calls=%fused_computation.12.clone.1 | convolution fusion | flops 1613234176 | bytes 14745728 | tf_op jit(solution)/shard_map/while/body/eval_jaxpr/hts,shp->thp/dot_general | solution.py:123
  479.3 2.2 copy.261
  481.5 45.6 %dynamic_update_slice.14 = f32[3,256,32,64]{1,0,3,2:T(4,128)} dynamic-update-slice(f32[3,256,32,64]{1,0,3,2:T(4,128)} %get-tuple-element.441, f32[1,256,32,64]{1,0,3,2:T(1,128)S(1)} %copy.261, s32[]{:T(128)} %get-tuple-element.439, s32[]{:T(128)} %constant.88.clone.1..sunk, s32[]{:T(128)} %constant.88.clone.1..sunk, s32[]{:T(128)} %constant.88.clone.1..sunk) | dynamic-update-slice | bytes 4194308 | tf_op jit(solution)/shard_map/while/body/jit(dynamic_update_index_in_dim)/dynamic_update_slice | solution.py:223
  533.6 2.9 fusion.146
  536.5 2.7 bitcast_add_fusion.2
  544.3 1.9 bitcast_multiply_fusion.4
  546.3 8.0 %fusion.149 = f32[1,256,32,64]{1,3,2,0:T(8,128)S(1)} fusion(f32[256,32,64]{0,2,1:T(8,128)S(1)} %bitcast.224, f32[4,256,8,64]{1,3,2,0:T(8,128)S(1)} %fusion.147, f32[32,256,256]{2,1,0:T(8,128)S(1)} %bitcast_multiply_fusion.4, f32[32]{0:T(128)S(1)} %get-tuple-element.461, f32[256,32]{0,1:T(8,128)S(1)} %get-tuple-element.420, f32[256,32]{0,1:T(8,128)S(1)} %bitcast.238), kind=kOutput, calls=%fused_computation.12.clone.1 | convolution fusion | flops 1613234176 | bytes 14745728 | tf_op jit(solution)/shard_map/while/body/eval_jaxpr/hts,shp->thp/dot_general | solution.py:123
  554.3 2.2 copy.261
  556.5 45.6 %dynamic_update_slice.14 = f32[3,256,32,64]{1,0,3,2:T(4,128)} dynamic-update-slice(f32[3,256,32,64]{1,0,3,2:T(4,128)} %get-tuple-element.441, f32[1,256,32,64]{1,0,3,2:T(1,128)S(1)} %copy.261, s32[]{:T(128)} %get-tuple-element.439, s32[]{:T(128)} %constant.88.clone.1..sunk, s32[]{:T(128)} %constant.88.clone.1..sunk, s32[]{:T(128)} %constant.88.clone.1..sunk) | dynamic-update-slice | bytes 4194308 | tf_op jit(solution)/shard_map/while/body/jit(dynamic_update_index_in_dim)/dynamic_update_slice | solution.py:223
  602.9 2.1 convert_element_type.127
  613.2 43.0 %all-reduce = bf16[512]{0:T(512)(128)(2,1)S(1)} all-reduce(bf16[512]{0:T(512)(128)(2,1)S(1)} %dynamic-update-slice), channel_id=2, replica_groups=mesh['tm'=16,'head'=2] {'tm'}, use_global_device_ids=true, to_apply=%add | all-reduce | flops 512 | bytes 2048
  656.3 7.6 copy.176
  663.9 55.5 %all-gather.10.cloned.1.call-done = bf16[512,64,128]{2,1,0:T(8,128)(2,1)} async-done(((bf16[32,64,128]{2,1,0:T(8,128)(2,1)}), bf16[512,64,128]{2,1,0:T(8,128)(2,1)}) %all-gather.10.cloned.1.call-update) | async-done | bytes 8388624 | tf_op jit(solution)/shard_map/all_gather | solution.py:18
  719.4 21.4 %while.30 = (s32[]{:T(128)}, f32[32,64,128]{2,1,0:T(8,128)S(1)}, s32[]{:T(128)}, bf16[16,32]{1,0:T(8,128)(2,1)S(1)}, bf16[16,32,64,128]{3,2,1,0:T(8,128)(2,1)}, /*index=5*/s32[]{:T(128)}, s32[]{:T(128)}) while((s32[]{:T(128)}, f32[32,64,128]{2,1,0:T(8,128)S(1)}, s32[]{:T(128)}, bf16[16,32]{1,0:T(8,128)(2,1)S(1)}, ...), condition=%wide.region_15.16_spmd.clone, body=%wide.region_14.15_spmd.clone.sunk | while | flops 1310756 | bytes 2621865 | solution.py:35
  740.8 4.4 fusion.76
  745.3 10.7 %reshape.282 = f32[3,256,32,64]{1,0,3,2:T(4,128)} reshape(f32[768,4,8,64]{0,3,2,1:T(8,128)} %bitcast.226) | data formatting | bytes 12582912 | tf_op jit(solution)/shard_map/reshape | solution.py:237
  756.0 10.0 %multiply_reduce_fusion.1 = f32[3,256,32]{1,0,2:T(4,128)S(1)} fusion(f32[3,256,32,64]{1,0,3,2:T(4,128)} %get-tuple-element.150, f32[3,256,32,64]{1,0,3,2:T(4,128)} %reshape.282, f32[3,256,32]{1,0,2:T(4,128)S(1)} %copy.139), kind=kLoop, calls=%fused_computation.54 | loop fusion | flops 6266880 | bytes 12779520 | tf_op jit(solution)/shard_map/reduce_sum | solution.py:152
  766.2 7.0 fusion.29
  773.1 4.6 copy.142
  (190 shorter events, 63.6 us)
Async XLA Ops:
  7.2 141.8 %copy-start = (bf16[576,1152]{1,0:T(8,128)(2,1)S(1)}, bf16[576,1152]{1,0:T(8,128)(2,1)}, u32[]{:S(2)}) copy-start(bf16[576,1152]{1,0:T(8,128)(2,1)} %param.25) | copy-start | bytes 3981316
  7.2 23.0 %all-gather.6.cloned.1.call-start = ((), (), s32[]{:S(2)}) async-start(), calls=%async_computation.2 | async-start | bytes 10616832 | tf_op jit(solution)/shard_map/all_gather | solution.py:181
  7.9 186.6 %all-reduce.3.cloned.1.call-start = ((), (), s32[]{:S(2)}) async-start(), calls=%async_computation.3 | async-start | bytes 7077888 | tf_op jit(solution)/shard_map/psum | solution.py:186
  40.5 5.0 copy-start.2
  40.5 7.1 copy-start.10
  157.6 2.3 copy-start.14
  160.7 50.9 %all-to-all-start = ((s32[16,1,1]{2,1,0:T(1,128)}), s32[16,1,1]{2,1,0:T(1,128)S(1)}, u32[]{:S(2)}, u32[]{:S(2)}) async-start(s32[16,1,1]{2,1,0:T(1,128)} %copy.120), calls=%async_computation | async-start | bytes 16384 | tf_op jit(solution)/shard_map/all_to_all | solution.py:202
  211.5 86.7 %all-to-all-start.1 = ((bf16[16,64,2048]{2,1,0:T(8,128)(2,1)}), bf16[16,64,2048]{2,1,0:T(8,128)(2,1)}, u32[]{:S(2)}, u32[]{:S(2)}) async-start(bf16[16,64,2048]{2,1,0:T(8,128)(2,1)} %copy.129), calls=%async_computation.1 | async-start | bytes 8388608 | tf_op jit(solution)/shard_map/all_to_all | solution.py:201
  218.5 121.5 %all-gather.8.cloned.1.call-start = ((), (), s32[]{:S(2)}) async-start(), calls=%async_computation.4 | async-start | bytes 9437184 | tf_op jit(solution)/shard_map/all_gather | solution.py:205
  305.2 3.7 copy-start.15
  308.6 35.7 %copy-start.12 = (bf16[4096,32]{0,1:T(8,128)(2,1)S(1)}, bf16[4096,32]{0,1:T(8,128)(2,1)}, u32[]{:S(2)}) copy-start(bf16[4096,32]{0,1:T(8,128)(2,1)} %param.31) | copy-start | bytes 786436
  308.6 35.7 %copy-start.13 = (f32[4096]{0:T(1024)S(1)}, f32[4096]{0:T(1024)}, u32[]{:S(2)}) copy-start(f32[4096]{0:T(1024)} %param.27) | copy-start | bytes 49156
  308.6 35.7 %copy-start.16 = (f32[32]{0:T(128)S(1)}, f32[32]{0:T(128)}, u32[]{:S(2)}) copy-start(f32[32]{0:T(128)} %param.32) | copy-start | bytes 388
  308.6 410.8 %all-gather.10.cloned.1.call-start = ((), (), s32[]{:S(2)}) async-start(), calls=%async_computation.5 | async-start | bytes 8912896 | tf_op jit(solution)/shard_map/all_gather | solution.py:18
  340.0 4.6 copy-start.3
  344.6 10.8 %slice-start = ((s8[6291456]{0:T(1024)(128)(4,1)}), s8[2097152]{0:T(1024)(128)(4,1)S(1)}, s32[]{:S(2)}) async-start(s8[6291456]{0:T(1024)(128)(4,1)} %bitcast.240), calls=%async_computation.6 | async-start | bytes 4194304
  346.9 8.5 %slice-start.1 = ((s8[6291456]{0:T(1024)(128)(4,1)}), s8[4194304]{0:T(1024)(128)(4,1)S(1)}, s32[]{:S(2)}) async-start(s8[6291456]{0:T(1024)(128)(4,1)} %bitcast.240), calls=%async_computation.7 | async-start | bytes 8388608
  346.9 8.5 %copy-start.11 = (bf16[4096,512]{1,0:T(8,128)(2,1)S(1)}, bf16[4096,512]{1,0:T(8,128)(2,1)}, u32[]{:S(2)}) copy-start(bf16[4096,512]{1,0:T(8,128)(2,1)} %param.29) | copy-start | bytes 12582916
  359.8 17.9 %copy-start.8 = (f32[32]{0:T(128)S(1)}, f32[32]{0:T(128)}, u32[]{:S(2)}) copy-start(f32[32]{0:T(128)} %param.34) | copy-start | bytes 388
  378.2 1.9 copy-start.6
  378.2 3.6 copy-start.4
  404.4 48.5 %copy-start.5 = (f32[3,256,32]{1,0,2:T(4,128)S(1)}, f32[3,256,32]{1,0,2:T(4,128)}, u32[]{:S(2)}) copy-start(f32[3,256,32]{1,0,2:T(4,128)} %copy-done.4) | copy-start | bytes 294916 | tf_op jit(solution)/shard_map/while
  404.4 48.5 %copy-start.7 = (f32[3,256,32]{1,0,2:T(4,128)S(1)}, f32[3,256,32]{1,0,2:T(4,128)}, u32[]{:S(2)}) copy-start(f32[3,256,32]{1,0,2:T(4,128)} %copy-done.6) | copy-start | bytes 294916 | tf_op jit(solution)/shard_map/while
  452.9 1.9 copy-start.6
  452.9 3.6 copy-start.4
  479.3 48.5 %copy-start.5 = (f32[3,256,32]{1,0,2:T(4,128)S(1)}, f32[3,256,32]{1,0,2:T(4,128)}, u32[]{:S(2)}) copy-start(f32[3,256,32]{1,0,2:T(4,128)} %copy-done.4) | copy-start | bytes 294916 | tf_op jit(solution)/shard_map/while
  479.3 48.5 %copy-start.7 = (f32[3,256,32]{1,0,2:T(4,128)S(1)}, f32[3,256,32]{1,0,2:T(4,128)}, u32[]{:S(2)}) copy-start(f32[3,256,32]{1,0,2:T(4,128)} %copy-done.6) | copy-start | bytes 294916 | tf_op jit(solution)/shard_map/while
  527.8 1.9 copy-start.6
  527.8 3.6 copy-start.4
  554.3 48.5 %copy-start.5 = (f32[3,256,32]{1,0,2:T(4,128)S(1)}, f32[3,256,32]{1,0,2:T(4,128)}, u32[]{:S(2)}) copy-start(f32[3,256,32]{1,0,2:T(4,128)} %copy-done.4) | copy-start | bytes 294916 | tf_op jit(solution)/shard_map/while
  554.3 48.5 %copy-start.7 = (f32[3,256,32]{1,0,2:T(4,128)S(1)}, f32[3,256,32]{1,0,2:T(4,128)}, u32[]{:S(2)}) copy-start(f32[3,256,32]{1,0,2:T(4,128)} %copy-done.6) | copy-start | bytes 294916 | tf_op jit(solution)/shard_map/while
  756.0 10.1 %copy-start.9 = (f32[2048]{0:T(1024)S(1)}, f32[2048]{0:T(1024)}, u32[]{:S(2)}) copy-start(f32[2048]{0:T(1024)} %param.35) | copy-start | bytes 24580
  766.2 11.6 %copy-start.1 = (bf16[576,1152]{1,0:T(8,128)(2,1)S(1)}, bf16[576,1152]{1,0:T(8,128)(2,1)}, u32[]{:S(2)}) copy-start(bf16[576,1152]{1,0:T(8,128)(2,1)} %param.25) | copy-start | bytes 3981316
Sparse Core Ops, SparseCore 0:
  9.5 20.6 all-gather.5
  159.9 25.2 all-reduce.2
  308.7 31.2 all-gather.7
  605.2 114.1 all-gather.9
where the time goes:
time: 799 us; the launch traced here: 784 us
  local copies, waits for them, and re-layouts  267 us (33%)
  waiting for transfers between devices  188 us (24%)
  matrix products  158 us (20%)
  other arithmetic  97.5 us (12%)
  blocking collectives  43 us (5%)
  between operations  15 us (2%)
  starting transfers between devices  14.1 us (2%)
    dynamic_update_slice x6, local copies, waits for them, and re-layouts, on_device(): device_state, (outputs, cumul) = lax.scan(stretch_step, zero_state, sliced)  143 us
    all_to_all x1, waiting for transfers between devices, on_device(): lax.all_to_all(outgoing, 'tm', split_axis=0, concat_axis=0, tiled=True)  79.3 us
    all_gather x1, waiting for transfers between devices, carried_in(): lax.all_gather(part.astype(kind), axis)  55.5 us
    unnamed x1, blocking collectives  43 us
    all_gather x1, waiting for transfers between devices, on_device(): wide = lax.all_gather(stream_rows, 'head', axis=1, tiled=True)  31.1 us
    dot_general x3, matrix products, ssd_stretch(): within = jnp.einsum('hts,shp->thp', mixing, scaled, precision=highest)  24 us
    dot_general x1, matrix products, attend(): jnp.einsum('fhqk,fkhd->fqhd', weights_soft, triple[2], preferred_element_...  21.9 us
    all_gather x1, waiting for transfers between devices, on_device(): full_patches = lax.all_gather(patches, 'head', axis=2, tiled=True)  21.5 us
  transfers between devices with their start and end apart: 6, of which 4 were waited for; matrix products, arithmetic and copies ran while one was open for 8% of the time, Pallas kernels for 0%

commit v1 on v0

--- a/solution.py
+++ b/solution.py
@@ -10,6 +10,22 @@
 STATE = 128
 STRETCH = 256
 highest = lax.Precision.HIGHEST
+
+
+def swapped_with_each(shard, axis, split, join):
+    ways, here = (lax.axis_size(axis), lax.axis_index(axis))
+    width = shard.shape[split] // ways
+    lengths = list(shard.shape)
+    lengths[split] = width
+    height = lengths[join]
+    lengths[join] = height * ways
+    full = jnp.zeros(lengths, shard.dtype)
+    for mask in range(ways):
+        part = lax.dynamic_slice_in_dim(shard, (here ^ mask) * width, width, axis=split)
+        if mask:
+            part = lax.ppermute(part, axis, [(d, d ^ mask) for d in range(ways)])
+        full = lax.dynamic_update_slice_in_dim(full, part, (here ^ mask) * height, axis=join)
+    return full
 
 
 def carried_in(value, axis, combine, identity):
@@ -198,7 +214,7 @@
         projected.reshape(frame_count, tokens_frame, w_conn.shape[1]), frame_ids, shards
     )
     incoming, arrived = (
-        lax.all_to_all(outgoing, "tm", split_axis=0, concat_axis=0, tiled=True),
+        swapped_with_each(outgoing, "tm", 0, 0),
         lax.all_to_all(labels, "tm", split_axis=0, concat_axis=0, tiled=True),
     )
     stream_rows = place_frames(incoming, arrived, frame_count)

time: 799 us -> 1100 us (1.38)
  local copies, waits for them, and re-layouts: 267 us -> 442 us
  waiting for transfers between devices: 188 us -> 275 us
  starting transfers between devices: 14.1 us -> 55.3 us
    dynamic_update_slice x0 -> x16, local copies, waits for them, and re-layouts: none -> 163 us  [swapped_with_each(): lax.dynamic_update_slice_in_dim(full, part, (here ^ mask) * height, axis=...]
    ppermute x0 -> x15, waiting for transfers between devices: none -> 132 us  [swapped_with_each(): part = lax.ppermute(part, axis, [(d, d ^ mask) for d in range(ways)])]
    all_to_all x1 -> x0, waiting for transfers between devices: 79.3 us -> none  [on_device(): lax.all_to_all(outgoing, 'tm', split_axis=0, concat_axis=0, tiled=True)]
    all_to_all x1, waiting for transfers between devices: 0.01 us -> 49.1 us  [on_device(): lax.all_to_all(labels, 'tm', split_axis=0, concat_axis=0, tiled=True)]
    ppermute x0 -> x15, starting transfers between devices: none -> 37.8 us  [swapped_with_each(): part = lax.ppermute(part, axis, [(d, d ^ mask) for d in range(ways)])]
    all_gather x1, waiting for transfers between devices: 31.1 us -> 16.3 us  [on_device(): wide = lax.all_gather(stream_rows, 'head', axis=1, tiled=True)]
    dynamic_slice x0 -> x1, local copies, waits for them, and re-layouts: none -> 13.7 us  [swapped_with_each(): lax.dynamic_slice_in_dim(shard, (here ^ mask) * width, width, axis=split)]
  transfers between devices with their start and end apart: 6 -> 20, of which waited for: 4 -> 12; matrix products, arithmetic and copies ran while one was open for 8% -> 18% of each run, Pallas kernels for 0% -> 0%
where the time goes in v1:
time: 1100 us; the launch traced here: 1080 us
  local copies, waits for them, and re-layouts  442 us (40%)
  waiting for transfers between devices  275 us (25%)
  matrix products  154 us (14%)
  other arithmetic  97.7 us (9%)
  starting transfers between devices  55.3 us (5%)
  blocking collectives  42.9 us (4%)
  between operations  15.1 us (1%)
    dynamic_update_slice x16, local copies, waits for them, and re-layouts, swapped_with_each(): lax.dynamic_update_slice_in_dim(full, part, (here ^ mask) * height, axis=...  163 us
    dynamic_update_slice x6, local copies, waits for them, and re-layouts, on_device(): device_state, (outputs, cumul) = lax.scan(stretch_step, zero_state, sliced)  143 us
    ppermute x15, waiting for transfers between devices, swapped_with_each(): part = lax.ppermute(part, axis, [(d, d ^ mask) for d in range(ways)])  132 us
    all_gather x1, waiting for transfers between devices, carried_in(): lax.all_gather(part.astype(kind), axis)  55.5 us
    all_to_all x1, waiting for transfers between devices, on_device(): lax.all_to_all(labels, 'tm', split_axis=0, concat_axis=0, tiled=True)  49.1 us
    unnamed x1, blocking collectives  42.9 us
    ppermute x15, starting transfers between devices, swapped_with_each(): part = lax.ppermute(part, axis, [(d, d ^ mask) for d in range(ways)])  37.8 us
    dot_general x3, matrix products, ssd_stretch(): within = jnp.einsum('hts,shp->thp', mixing, scaled, precision=highest)  24 us
  transfers between devices with their start and end apart: 20, of which 12 were waited for; matrix products, arithmetic and copies ran while one was open for 18% of the time, Pallas kernels for 0%

profile of v1, /device:TPU:0, one launch (start us, length us, event | category | flops | bytes accessed | tf_op | source)
XLA Modules:
  0.0 1083.7 jit_solution(17535358395331710314)
XLA Ops:
  8.7 21.5 %all-gather.6.cloned.1.call-done = bf16[12,256,1152]{1,2,0:T(8,128)(2,1)} async-done(((bf16[12,256,576]{1,2,0:T(8,128)(2,1)}), bf16[12,256,1152]{1,2,0:T(8,128)(2,1)}) %all-gather.6.cloned.1.call-update) | async-done | bytes 7077904 | tf_op jit(solution)/shard_map/all_gather | solution.py:197
  30.2 10.3 copy.121
  40.5 4.2 convert_reduce_fusion
  50.0 15.7 %convert_bitcast_fusion = bf16[3,3072,576]{1,2,0:T(8,128)(2,1)S(1)} fusion(bf16[3072,1152,1]{1,0,2:T(8,128)(2,1)S(1)} %bitcast.240, bf16[3,1152,576]{1,2,0:T(8,128)(2,1)} %param.24), kind=kOutput, calls=%fused_computation.52 | convolution fusion | flops 12235898880 | bytes 21676032 | tf_op jit(solution)/shard_map/rc,mcd->mrd/dot_general | solution.py:66
  65.7 4.1 fusion.91
  69.9 7.2 squeeze.32
  77.1 7.3 squeeze.33
  84.5 7.2 squeeze.31
  91.7 15.7 %fusion.92 = f32[12,8,256]{2,1,0:T(8,128)S(1)} fusion(pred[12,256]{1,0:T(8,128)(4,1)S(1)} %iota_compare_fusion.1, bf16[12,256,8,72]{1,0,3,2:T(8,128)(2,1)} %squeeze.33, bf16[12,256,8,72]{1,0,3,2:T(8,128)(2,1)} %squeeze.32), kind=kOutput, calls=%fused_computation.134 | convolution fusion | flops 931135744 | bytes 7179264 | tf_op jit(solution)/shard_map/sub | solution.py:76
  107.4 21.9 %convert_bitcast_fusion.1 = bf16[12,256,8,72]{1,3,2,0:T(8,128)(2,1)} fusion(f32[12,8,256]{2,1,0:T(8,128)S(1)} %fusion.92, pred[12,256]{1,0:T(8,128)(4,1)S(1)} %iota_compare_fusion.1, bf16[12,256,8,72]{1,0,3,2:T(8,128)(2,1)} %squeeze.31, bf16[12,256,8,72]{1,0,3,2:T(8,128)(2,1)} %squeeze.33, bf16[12,256,8,72]{1,0,3,2:T(8,128)(2,1)} %squeeze.32), kind=kOutput, calls=%fused_computation.69 | convolution fusion | flops 1845190912 | bytes 14257152 | tf_op jit(solution)/shard_map/fhqk,fkhd->fqhd/dot_general | solution.py:78
  129.3 8.0 copy.126
  137.3 11.6 %dot_general.53 = bf16[12,64,4,576]{3,2,1,0:T(4,128)(2,1)} reshape(bf16[12,256,8,72]{3,2,1,0:T(8,128)(2,1)} %copy.126) | data formatting | bytes 7077888 | tf_op jit(solution)/shard_map/dot_general | solution.py:81
  148.9 8.6 fusion.44
  160.0 13.9 %reshape.268 = f32[12,64,4,1152]{3,2,1,0:T(4,128)} reshape(bf16[12,256,1152]{2,1,0:T(8,128)(2,1)} %copy.121) | data formatting | bytes 21233664 | tf_op jit(solution)/shard_map/reshape | solution.py:204
  174.0 13.2 %reduce_sum.89 = f32[12,64,1152]{2,1,0:T(8,128)} reduce(f32[12,64,4,1152]{3,2,1,0:T(4,128)} %reshape.268, f32[]{:T(128)} %constant.111.clone.1), dimensions={2}, to_apply=%region_1.0 | reduce | flops 2654208 | bytes 17694724 | tf_op jit(solution)/shard_map/reduce_sum | solution.py:203
  190.7 6.9 convolution_convert_fusion.2
  200.0 13.7 %constant_dynamic-slice_fusion.5 = (bf16[1,64,2048]{2,0,1:T(2,128)(2,1)}, bf16[1,64,2048]{2,0,1:T(2,128)(2,1)}, bf16[1,64,2048]{2,0,1:T(2,128)(2,1)}, bf16[1,64,...) fusion(bf16[16,64,2048]{2,0,1:T(8,128)(2,1)S(1)} %fusion.36, ...), kind=kLoop, calls=%fused_computation.107 | loop fusion | bytes 8388672 | tf_op jit(solution)/shard_map/dynamic_slice | solution.py:24
  220.3 8.1 collective-permute-done
  233.0 25.0 %collective-permute-done.2 = bf16[1,64,2048]{2,0,1:T(2,128)(2,1)S(1)} collective-permute-done((bf16[1,64,2048]{2,0,1:T(2,128)(2,1)S(1)}, bf16[1,64,2048]{2,0,1:T(2,128)(2,1)S(1)}, u32[]{:S(2)}, u32[]{:S(2)}) %collective-permute-start.2) | collective-permute-done | bytes 262176 | tf_op jit(solution)/shard_map/ppermute | solution.py:26
  264.7 12.2 %collective-permute-done.5 = bf16[1,64,2048]{2,0,1:T(2,128)(2,1)} collective-permute-done((bf16[1,64,2048]{2,0,1:T(2,128)(2,1)S(1)}, bf16[1,64,2048]{2,0,1:T(2,128)(2,1)}, u32[]{:S(2)}, u32[]{:S(2)}) %collective-permute-start.5) | collective-permute-done | bytes 262176 | tf_op jit(solution)/shard_map/ppermute | solution.py:26
  276.9 10.2 collective-permute-done.6
  288.6 47.0 %collective-permute-done.7 = bf16[1,64,2048]{2,0,1:T(2,128)(2,1)} collective-permute-done((bf16[1,64,2048]{2,0,1:T(2,128)(2,1)S(1)}, bf16[1,64,2048]{2,0,1:T(2,128)(2,1)}, u32[]{:S(2)}, u32[]{:S(2)}) %collective-permute-start.7) | collective-permute-done | bytes 262176 | tf_op jit(solution)/shard_map/ppermute | solution.py:26
  335.6 4.7 collective-permute-start.12
  340.3 25.2 %collective-permute-done.8 = bf16[1,64,2048]{2,0,1:T(2,128)(2,1)} collective-permute-done((bf16[1,64,2048]{2,0,1:T(2,128)(2,1)S(1)}, bf16[1,64,2048]{2,0,1:T(2,128)(2,1)}, u32[]{:S(2)}, u32[]{:S(2)}) %collective-permute-start.8) | collective-permute-done | bytes 262176 | tf_op jit(solution)/shard_map/ppermute | solution.py:26
  368.9 14.3 %collective-permute-start.14 = (bf16[1,64,2048]{2,0,1:T(2,128)(2,1)}, bf16[1,64,2048]{2,0,1:T(2,128)(2,1)}, u32[]{:S(2)}, u32[]{:S(2)}) collective-permute-start(bf16[1,64,2048]{2,0,1:T(2,128)(2,1)} %get-tuple-element.308), channel_id=1, source_target_pairs={{0,30},{2,28},{4,26},{6,24},{8,22},{10,20},{12,18},{14,16},{16,14}... | collective-permute-start | bytes 786440 | tf_op jit(solution)/shard_map/ppermute | solution.py:26
  384.0 16.9 %all-to-all-start = ((s32[16,1,1]{2,1,0:T(1,128)}), s32[16,1,1]{2,1,0:T(1,128)S(1)}, u32[]{:S(2)}, u32[]{:S(2)}) async-start(s32[16,1,1]{2,1,0:T(1,128)} %copy.120), calls=%async_computation | async-start | bytes 16384 | tf_op jit(solution)/shard_map/all_to_all | solution.py:218
  400.9 49.1 %all-to-all-done = s32[16,1,1]{2,1,0:T(1,128)S(1)} async-done(((s32[16,1,1]{2,1,0:T(1,128)}), s32[16,1,1]{2,1,0:T(1,128)S(1)}, u32[]{:S(2)}, u32[]{:S(2)}) %all-to-all-start) | async-done | bytes 96 | tf_op jit(solution)/shard_map/all_to_all | solution.py:218
  452.9 10.2 dynamic_update_slice.56
  463.1 10.2 dynamic_update_slice.57
  473.3 10.2 dynamic_update_slice.58
  483.4 10.2 dynamic_update_slice.59
  493.6 10.2 dynamic_update_slice.60
  503.8 10.2 dynamic_update_slice.61
  513.9 10.2 dynamic_update_slice.62
  524.1 10.2 dynamic_update_slice.63
  534.3 10.2 dynamic_update_slice.64
  544.5 10.2 dynamic_update_slice.65
  554.7 10.2 dynamic_update_slice.66
  564.9 10.2 dynamic_update_slice.67
  575.1 10.2 dynamic_update_slice.68
  585.3 10.2 dynamic_update_slice.69
  595.6 10.2 dynamic_update_slice.70
  605.8 10.2 dynamic_update_slice.71
  623.3 16.3 %all-gather.8.cloned.1.call-done = bf16[768,4096]{1,0:T(8,128)(2,1)} async-done(((bf16[768,2048]{1,0:T(8,128)(2,1)}), bf16[768,4096]{1,0:T(8,128)(2,1)}) %all-gather.8.cloned.1.call-update) | async-done | bytes 6291472 | tf_op jit(solution)/shard_map/all_gather | solution.py:221
  639.6 4.2 fusion.19
  646.5 8.5 convolution_convert_fusion.3
  655.0 4.4 convolution_convert_fusion.4
  659.4 17.9 %convolution_convert_fusion.1 = bf16[768,2048]{1,0:T(8,128)(2,1)} fusion(bf16[4096,2048]{1,0:T(8,128)(2,1)} %param.28, bf16[768,4096]{1,0:T(8,128)(2,1)S(1)} %bitcast.242, f32[4096]{0:T(1024)S(1)} %copy-done.13, f32[768]{0:T(1024)S(1)} %add_rsqrt_fusion.2), kind=kOutput, calls=%fused_computation.70 | convolution fusion | flops 12899057664 | bytes 26233856 | tf_op jit(solution)/shard_map/dot_general | solution.py:115
  677.3 224.9 %while.29 = (s32[]{:T(128)}, f32[32,64,128]{2,1,0:T(8,128)}, f32[3,256,32,64]{1,0,3,2:T(4,128)}, f32[3,256,32]{1,2,0:T(8,128)}, f32[3,256,32]{1,0,2:T(4,128)S(1)...) while((s32[]{:T(128)}, f32[32,64,128]{2,1,0:T(8,128)}, ...), condition=%wide.region_12.13_spmd.clone, body=%wide.region_9.12_spmd.clone.sunk | while | flops 3302842368 | bytes 56987660 | solution.py:239
  695.6 8.0 fusion.145
  705.8 45.6 %dynamic_update_slice.78 = f32[3,256,32,64]{1,0,3,2:T(4,128)} dynamic-update-slice(f32[3,256,32,64]{1,0,3,2:T(4,128)} %get-tuple-element.457, f32[1,256,32,64]{1,0,3,2:T(1,128)S(1)} %copy.255, s32[]{:T(128)} %get-tuple-element.455, s32[]{:T(128)} %constant.60.clone.1..sunk, s32[]{:T(128)} %constant.60.clone.1..sunk, s32[]{:T(128)} %constant.60.clone.1..sunk) | dynamic-update-slice | bytes 4194308 | tf_op jit(solution)/shard_map/while/body/jit(dynamic_update_index_in_dim)/dynamic_update_slice | solution.py:239
  770.6 8.0 fusion.145
  780.8 45.6 %dynamic_update_slice.78 = f32[3,256,32,64]{1,0,3,2:T(4,128)} dynamic-update-slice(f32[3,256,32,64]{1,0,3,2:T(4,128)} %get-tuple-element.457, f32[1,256,32,64]{1,0,3,2:T(1,128)S(1)} %copy.255, s32[]{:T(128)} %get-tuple-element.455, s32[]{:T(128)} %constant.60.clone.1..sunk, s32[]{:T(128)} %constant.60.clone.1..sunk, s32[]{:T(128)} %constant.60.clone.1..sunk) | dynamic-update-slice | bytes 4194308 | tf_op jit(solution)/shard_map/while/body/jit(dynamic_update_index_in_dim)/dynamic_update_slice | solution.py:239
  845.5 8.0 fusion.145
  855.7 45.6 %dynamic_update_slice.78 = f32[3,256,32,64]{1,0,3,2:T(4,128)} dynamic-update-slice(f32[3,256,32,64]{1,0,3,2:T(4,128)} %get-tuple-element.457, f32[1,256,32,64]{1,0,3,2:T(1,128)S(1)} %copy.255, s32[]{:T(128)} %get-tuple-element.455, s32[]{:T(128)} %constant.60.clone.1..sunk, s32[]{:T(128)} %constant.60.clone.1..sunk, s32[]{:T(128)} %constant.60.clone.1..sunk) | dynamic-update-slice | bytes 4194308 | tf_op jit(solution)/shard_map/while/body/jit(dynamic_update_index_in_dim)/dynamic_update_slice | solution.py:239
  912.4 42.9 %all-reduce = bf16[512]{0:T(512)(128)(2,1)S(1)} all-reduce(bf16[512]{0:T(512)(128)(2,1)S(1)} %dynamic-update-slice), channel_id=2, replica_groups=mesh['tm'=16,'head'=2] {'tm'}, use_global_device_ids=true, to_apply=%add | all-reduce | flops 512 | bytes 2048
  955.4 7.6 copy.174
  963.0 55.5 %all-gather.10.cloned.1.call-done = bf16[512,64,128]{2,1,0:T(8,128)(2,1)} async-done(((bf16[32,64,128]{2,1,0:T(8,128)(2,1)}), bf16[512,64,128]{2,1,0:T(8,128)(2,1)}) %all-gather.10.cloned.1.call-update) | async-done | bytes 8388624 | tf_op jit(solution)/shard_map/all_gather | solution.py:34
  1018.6 21.4 %while.30 = (s32[]{:T(128)}, f32[32,64,128]{2,1,0:T(8,128)S(1)}, s32[]{:T(128)}, bf16[16,32]{1,0:T(8,128)(2,1)S(1)}, bf16[16,32,64,128]{3,2,1,0:T(8,128)(2,1)}, /*index=5*/s32[]{:T(128)}, s32[]{:T(128)}) while((s32[]{:T(128)}, f32[32,64,128]{2,1,0:T(8,128)S(1)}, s32[]{:T(128)}, bf16[16,32]{1,0:T(8,128)(2,1)S(1)}, ...), condition=%wide.region_15.16_spmd.clone, body=%wide.region_14.15_spmd.clone.sunk | while | flops 1310756 | bytes 2621865 | solution.py:51
  1040.0 4.5 fusion.71
  1044.4 10.7 reshape.282
  1055.2 10.0 multiply_reduce_fusion.1
  1065.3 7.0 fusion.29
  1072.3 4.6 copy.140
  (235 shorter events, 145.4 us)
Async XLA Ops:
  7.2 141.8 %copy-start = (bf16[576,1152]{1,0:T(8,128)(2,1)S(1)}, bf16[576,1152]{1,0:T(8,128)(2,1)}, u32[]{:S(2)}) copy-start(bf16[576,1152]{1,0:T(8,128)(2,1)} %param.25) | copy-start | bytes 3981316
  7.2 23.0 %all-gather.6.cloned.1.call-start = ((), (), s32[]{:S(2)}) async-start(), calls=%async_computation.1 | async-start | bytes 10616832 | tf_op jit(solution)/shard_map/all_gather | solution.py:197
  7.9 179.3 %all-reduce.3.cloned.1.call-start = ((), (), s32[]{:S(2)}) async-start(), calls=%async_computation.2 | async-start | bytes 7077888 | tf_op jit(solution)/shard_map/psum | solution.py:202
  40.5 5.0 copy-start.2
  44.7 2.9 copy-start.10
  157.6 2.4 copy-start.14
  213.7 14.8 %collective-permute-start = (bf16[1,64,2048]{2,0,1:T(2,128)(2,1)S(1)}, bf16[1,64,2048]{2,0,1:T(2,128)(2,1)S(1)}, u32[]{:S(2)}, u32[]{:S(2)}) collective-permute-start(bf16[1,64,2048]{2,0,1:T(2,128)(2,1)S(1)} %get-tuple-element.322), channel_id=1, source_target_pairs={{0,2},{2,0},{4,6},{6,4},{8,10},{10,8},{12,14},{14,12},{16,18},{18,... | collective-permute-start | bytes 786440 | tf_op jit(solution)/shard_map/ppermute | solution.py:26
  215.4 16.4 %collective-permute-start.1 = (bf16[1,64,2048]{2,0,1:T(2,128)(2,1)S(1)}, bf16[1,64,2048]{2,0,1:T(2,128)(2,1)S(1)}, u32[]{:S(2)}, u32[]{:S(2)}) collective-permute-start(bf16[1,64,2048]{2,0,1:T(2,128)(2,1)S(1)} %get-tuple-element.321), channel_id=1, source_target_pairs={{0,4},{2,6},{4,0},{6,2},{8,12},{10,14},{12,8},{14,10},{16,20},{18,... | collective-permute-start | bytes 786440 | tf_op jit(solution)/shard_map/ppermute | solution.py:26
  216.9 41.1 %collective-permute-start.2 = (bf16[1,64,2048]{2,0,1:T(2,128)(2,1)S(1)}, bf16[1,64,2048]{2,0,1:T(2,128)(2,1)S(1)}, u32[]{:S(2)}, u32[]{:S(2)}) collective-permute-start(bf16[1,64,2048]{2,0,1:T(2,128)(2,1)S(1)} %get-tuple-element.320), channel_id=1, source_target_pairs={{0,6},{2,4},{4,2},{6,0},{8,14},{10,12},{12,10},{14,8},{16,22},{18,... | collective-permute-start | bytes 786440 | tf_op jit(solution)/shard_map/ppermute | solution.py:26
  217.1 43.3 %collective-permute-start.3 = (bf16[1,64,2048]{2,0,1:T(2,128)(2,1)S(1)}, bf16[1,64,2048]{2,0,1:T(2,128)(2,1)S(1)}, u32[]{:S(2)}, u32[]{:S(2)}) collective-permute-start(bf16[1,64,2048]{2,0,1:T(2,128)(2,1)S(1)} %get-tuple-element.319), channel_id=1, source_target_pairs={{0,8},{2,10},{4,12},{6,14},{8,0},{10,2},{12,4},{14,6},{16,24},{18,... | collective-permute-start | bytes 786440 | tf_op jit(solution)/shard_map/ppermute | solution.py:26
  218.9 43.4 %collective-permute-start.4 = (bf16[1,64,2048]{2,0,1:T(2,128)(2,1)S(1)}, bf16[1,64,2048]{2,0,1:T(2,128)(2,1)S(1)}, u32[]{:S(2)}, u32[]{:S(2)}) collective-permute-start(bf16[1,64,2048]{2,0,1:T(2,128)(2,1)S(1)} %get-tuple-element.318), channel_id=1, source_target_pairs={{0,10},{2,8},{4,14},{6,12},{8,2},{10,0},{12,6},{14,4},{16,26},{18,... | collective-permute-start | bytes 786440 | tf_op jit(solution)/shard_map/ppermute | solution.py:26
  228.5 48.4 %collective-permute-start.5 = (bf16[1,64,2048]{2,0,1:T(2,128)(2,1)S(1)}, bf16[1,64,2048]{2,0,1:T(2,128)(2,1)}, u32[]{:S(2)}, u32[]{:S(2)}) collective-permute-start(bf16[1,64,2048]{2,0,1:T(2,128)(2,1)S(1)} %get-tuple-element.317), channel_id=1, source_target_pairs={{0,12},{2,14},{4,8},{6,10},{8,4},{10,6},{12,0},{14,2},{16,28},{18,... | collective-permute-start | bytes 786440 | tf_op jit(solution)/shard_map/ppermute | solution.py:26
  231.8 55.3 %collective-permute-start.6 = (bf16[1,64,2048]{2,0,1:T(2,128)(2,1)S(1)}, bf16[1,64,2048]{2,0,1:T(2,128)(2,1)}, u32[]{:S(2)}, u32[]{:S(2)}) collective-permute-start(bf16[1,64,2048]{2,0,1:T(2,128)(2,1)S(1)} %get-tuple-element.316), channel_id=1, source_target_pairs={{0,14},{2,12},{4,10},{6,8},{8,6},{10,4},{12,2},{14,0},{16,30},{18,... | collective-permute-start | bytes 786440 | tf_op jit(solution)/shard_map/ppermute | solution.py:26
  258.0 77.6 %collective-permute-start.7 = (bf16[1,64,2048]{2,0,1:T(2,128)(2,1)S(1)}, bf16[1,64,2048]{2,0,1:T(2,128)(2,1)}, u32[]{:S(2)}, u32[]{:S(2)}) collective-permute-start(bf16[1,64,2048]{2,0,1:T(2,128)(2,1)S(1)} %get-tuple-element.315), channel_id=1, source_target_pairs={{0,16},{2,18},{4,20},{6,22},{8,24},{10,26},{12,28},{14,30},{16,0},... | collective-permute-start | bytes 786440 | tf_op jit(solution)/shard_map/ppermute | solution.py:26
  260.4 105.1 %collective-permute-start.8 = (bf16[1,64,2048]{2,0,1:T(2,128)(2,1)S(1)}, bf16[1,64,2048]{2,0,1:T(2,128)(2,1)}, u32[]{:S(2)}, u32[]{:S(2)}) collective-permute-start(bf16[1,64,2048]{2,0,1:T(2,128)(2,1)S(1)} %get-tuple-element.314), channel_id=1, source_target_pairs={{0,18},{2,16},{4,22},{6,20},{8,26},{10,24},{12,30},{14,28},{16,2},... | collective-permute-start | bytes 786440 | tf_op jit(solution)/shard_map/ppermute | solution.py:26
  262.3 106.6 %collective-permute-start.9 = (bf16[1,64,2048]{2,0,1:T(2,128)(2,1)S(1)}, bf16[1,64,2048]{2,0,1:T(2,128)(2,1)}, u32[]{:S(2)}, u32[]{:S(2)}) collective-permute-start(bf16[1,64,2048]{2,0,1:T(2,128)(2,1)S(1)} %get-tuple-element.313), channel_id=1, source_target_pairs={{0,20},{2,22},{4,16},{6,18},{8,28},{10,30},{12,24},{14,26},{16,4},... | collective-permute-start | bytes 786440 | tf_op jit(solution)/shard_map/ppermute | solution.py:26
  276.9 288.1 %collective-permute-start.10 = (bf16[1,64,2048]{2,0,1:T(2,128)(2,1)}, bf16[1,64,2048]{2,0,1:T(2,128)(2,1)}, u32[]{:S(2)}, u32[]{:S(2)}) collective-permute-start(bf16[1,64,2048]{2,0,1:T(2,128)(2,1)} %get-tuple-element.312), channel_id=1, source_target_pairs={{0,22},{2,20},{4,18},{6,16},{8,30},{10,28},{12,26},{14,24},{16,6},... | collective-permute-start | bytes 786440 | tf_op jit(solution)/shard_map/ppermute | solution.py:26
  287.0 288.1 %collective-permute-start.11 = (bf16[1,64,2048]{2,0,1:T(2,128)(2,1)}, bf16[1,64,2048]{2,0,1:T(2,128)(2,1)}, u32[]{:S(2)}, u32[]{:S(2)}) collective-permute-start(bf16[1,64,2048]{2,0,1:T(2,128)(2,1)} %get-tuple-element.311), channel_id=1, source_target_pairs={{0,24},{2,26},{4,28},{6,30},{8,16},{10,18},{12,20},{14,22},{16,8},... | collective-permute-start | bytes 786440 | tf_op jit(solution)/shard_map/ppermute | solution.py:26
  335.6 249.8 %collective-permute-start.12 = (bf16[1,64,2048]{2,0,1:T(2,128)(2,1)}, bf16[1,64,2048]{2,0,1:T(2,128)(2,1)}, u32[]{:S(2)}, u32[]{:S(2)}) collective-permute-start(bf16[1,64,2048]{2,0,1:T(2,128)(2,1)} %get-tuple-element.310), channel_id=1, source_target_pairs={{0,26},{2,24},{4,30},{6,28},{8,18},{10,16},{12,22},{14,20},{16,10}... | collective-permute-start | bytes 786440 | tf_op jit(solution)/shard_map/ppermute | solution.py:26
  365.5 230.1 %collective-permute-start.13 = (bf16[1,64,2048]{2,0,1:T(2,128)(2,1)}, bf16[1,64,2048]{2,0,1:T(2,128)(2,1)}, u32[]{:S(2)}, u32[]{:S(2)}) collective-permute-start(bf16[1,64,2048]{2,0,1:T(2,128)(2,1)} %get-tuple-element.309), channel_id=1, source_target_pairs={{0,28},{2,30},{4,24},{6,26},{8,20},{10,22},{12,16},{14,18},{16,12}... | collective-permute-start | bytes 786440 | tf_op jit(solution)/shard_map/ppermute | solution.py:26
  368.9 236.9 %collective-permute-start.14 = (bf16[1,64,2048]{2,0,1:T(2,128)(2,1)}, bf16[1,64,2048]{2,0,1:T(2,128)(2,1)}, u32[]{:S(2)}, u32[]{:S(2)}) collective-permute-start(bf16[1,64,2048]{2,0,1:T(2,128)(2,1)} %get-tuple-element.308), channel_id=1, source_target_pairs={{0,30},{2,28},{4,26},{6,24},{8,22},{10,20},{12,18},{14,16},{16,14}... | collective-permute-start | bytes 786440 | tf_op jit(solution)/shard_map/ppermute | solution.py:26
  384.0 66.1 %all-to-all-start = ((s32[16,1,1]{2,1,0:T(1,128)}), s32[16,1,1]{2,1,0:T(1,128)S(1)}, u32[]{:S(2)}, u32[]{:S(2)}) async-start(s32[16,1,1]{2,1,0:T(1,128)} %copy.120), calls=%async_computation | async-start | bytes 16384 | tf_op jit(solution)/shard_map/all_to_all | solution.py:218
  400.9 238.7 %all-gather.8.cloned.1.call-start = ((), (), s32[]{:S(2)}) async-start(), calls=%async_computation.3 | async-start | bytes 9437184 | tf_op jit(solution)/shard_map/all_gather | solution.py:221
  619.4 3.9 copy-start.15
  622.8 21.0 %copy-start.12 = (bf16[4096,32]{0,1:T(8,128)(2,1)S(1)}, bf16[4096,32]{0,1:T(8,128)(2,1)}, u32[]{:S(2)}) copy-start(bf16[4096,32]{0,1:T(8,128)(2,1)} %param.31) | copy-start | bytes 786436
  622.8 21.0 %copy-start.13 = (f32[4096]{0:T(1024)S(1)}, f32[4096]{0:T(1024)}, u32[]{:S(2)}) copy-start(f32[4096]{0:T(1024)} %param.27) | copy-start | bytes 49156
  622.8 21.1 %copy-start.16 = (f32[32]{0:T(128)S(1)}, f32[32]{0:T(128)}, u32[]{:S(2)}) copy-start(f32[32]{0:T(128)} %param.32) | copy-start | bytes 388
  622.8 395.7 %all-gather.10.cloned.1.call-start = ((), (), s32[]{:S(2)}) async-start(), calls=%async_computation.4 | async-start | bytes 8912896 | tf_op jit(solution)/shard_map/all_gather | solution.py:34
  639.6 4.6 copy-start.3
  644.2 10.8 slice-start
  646.5 8.5 slice-start.1
  646.5 8.5 copy-start.11
  659.4 17.9 %copy-start.8 = (f32[32]{0:T(128)S(1)}, f32[32]{0:T(128)}, u32[]{:S(2)}) copy-start(f32[32]{0:T(128)} %param.34) | copy-start | bytes 388
  677.5 1.9 copy-start.6
  677.5 3.6 copy-start.4
  703.6 48.5 %copy-start.5 = (f32[3,256,32]{1,0,2:T(4,128)S(1)}, f32[3,256,32]{1,0,2:T(4,128)}, u32[]{:S(2)}) copy-start(f32[3,256,32]{1,0,2:T(4,128)} %copy-done.4) | copy-start | bytes 294916 | tf_op jit(solution)/shard_map/while
  703.6 48.5 %copy-start.7 = (f32[3,256,32]{1,0,2:T(4,128)S(1)}, f32[3,256,32]{1,0,2:T(4,128)}, u32[]{:S(2)}) copy-start(f32[3,256,32]{1,0,2:T(4,128)} %copy-done.6) | copy-start | bytes 294916 | tf_op jit(solution)/shard_map/while
  752.1 1.9 copy-start.6
  752.2 3.6 copy-start.4
  778.6 48.5 %copy-start.5 = (f32[3,256,32]{1,0,2:T(4,128)S(1)}, f32[3,256,32]{1,0,2:T(4,128)}, u32[]{:S(2)}) copy-start(f32[3,256,32]{1,0,2:T(4,128)} %copy-done.4) | copy-start | bytes 294916 | tf_op jit(solution)/shard_map/while
  778.6 48.5 %copy-start.7 = (f32[3,256,32]{1,0,2:T(4,128)S(1)}, f32[3,256,32]{1,0,2:T(4,128)}, u32[]{:S(2)}) copy-start(f32[3,256,32]{1,0,2:T(4,128)} %copy-done.6) | copy-start | bytes 294916 | tf_op jit(solution)/shard_map/while
  827.1 1.9 copy-start.6
  827.1 3.6 copy-start.4
  853.6 48.5 %copy-start.5 = (f32[3,256,32]{1,0,2:T(4,128)S(1)}, f32[3,256,32]{1,0,2:T(4,128)}, u32[]{:S(2)}) copy-start(f32[3,256,32]{1,0,2:T(4,128)} %copy-done.4) | copy-start | bytes 294916 | tf_op jit(solution)/shard_map/while
  853.6 48.5 %copy-start.7 = (f32[3,256,32]{1,0,2:T(4,128)S(1)}, f32[3,256,32]{1,0,2:T(4,128)}, u32[]{:S(2)}) copy-start(f32[3,256,32]{1,0,2:T(4,128)} %copy-done.6) | copy-start | bytes 294916 | tf_op jit(solution)/shard_map/while
  1055.2 10.1 copy-start.9
  1065.3 11.6 %copy-start.1 = (bf16[576,1152]{1,0:T(8,128)(2,1)S(1)}, bf16[576,1152]{1,0:T(8,128)(2,1)}, u32[]{:S(2)}) copy-start(bf16[576,1152]{1,0:T(8,128)(2,1)} %param.25) | copy-start | bytes 3981316
Sparse Core Ops, SparseCore 0:
  9.5 20.6 all-gather.5
  159.9 25.2 all-reduce.2
  622.9 16.6 all-gather.7
  904.5 113.9 all-gather.9
